TPU v7x, 256 devices: a whole 4x4x8 slice. The times are simulated.
256 devices in a mesh: dp: 4 (over x), expert: 32 (over z, y), tensor: 2 (over core).
Axes of the slice: x: 4, y: 4, z: 8, core: 2. Of those that a mesh axis runs over, the one named last changes fastest.
Arguments:
- queries: bfloat16 [8192, 4096], P(('dp', 'expert'), 'tensor'), may hold values from -8 to 8
- fresh_keys: bfloat16 [8192, 512], P(('dp', 'expert'), 'tensor'), may hold values from -6 to 6
- fresh_values: bfloat16 [8192, 512], P(('dp', 'expert'), 'tensor'), may hold values from -6 to 6
- resident_keys: bfloat16 [128, 2048, 512], P(('dp', 'expert'), None, 'tensor'), may hold values from -8 to 8
- resident_values: bfloat16 [128, 2048, 512], P(('dp', 'expert'), None, 'tensor'), may hold values from -6 to 6
- out_weight: bfloat16 [4096, 2048], P('tensor', 'dp'), may hold values from -0.5 to 0.5
- residual: bfloat16 [8192, 2048], P(('dp', 'expert')), may hold values from -23 to 23
- norm_gain: float32 [2048], replicated, may hold values from 0.1 to 1.9
- expert_ids: int32 [8192, 8], P(('dp', 'expert')), may hold values from 0 to 127, all different within a row; in each aligned block of 64 rows (0 to 63, 64 to 127, ...) at most 6 rows name the same one
- gates: float32 [8192, 8], P(('dp', 'expert')), may hold values from 0.05 to 0.5
- w_gate: bfloat16 [128, 2048, 768], P(('dp', 'expert'), None, 'tensor'), may hold values from -0.125 to 0.125
- w_up: bfloat16 [128, 2048, 768], P(('dp', 'expert'), None, 'tensor'), may hold values from -0.125 to 0.125
- w_down: bfloat16 [128, 768, 2048], P(('dp', 'expert'), 'tensor'), may hold values from -0.21875 to 0.21875
Outputs:
- mixed: bfloat16 [8192, 2048], P(('dp', 'expert'), 'tensor')
Inputs may be any that keep to these rules, and one draw needn't show every extreme that they name: `expert_ids`: within the 64 tokens of one sequence no expert is named by more than 6 tokens, a bound that some block reaches; a token names 8 different experts.
All inputs are finite; a program needn't handle non-finite values.
Results may differ from a plain program's by a relative error of at most 0.0085.
Values may be sent and summed in bfloat16 or wider, within the bound.
No kernel may reach another device: no remote copies, remote signals or barrier semaphores. Data moves between devices by JAX's collectives and lax.ppermute only.
A program may use at most 64 MiB of HBM per device.

v0:
```python
import jax
import jax.numpy as jnp
from jax import lax
from jax.sharding import PartitionSpec as P

D = 2048
HEAD_WIDTH = 128
CAP = 6


def attend_local(queries, fresh_keys, fresh_values, resident_keys, resident_values):
    tokens_here = queries.shape[0]
    kv_here = fresh_keys.shape[1] // HEAD_WIDTH
    query_group = queries.shape[1] // HEAD_WIDTH // kv_here
    context = resident_keys.shape[1]
    query_rows = queries.reshape(tokens_here, kv_here, query_group, HEAD_WIDTH)
    joined_keys = jnp.concatenate([resident_keys[0], fresh_keys], 0).reshape(
        context + tokens_here, kv_here, HEAD_WIDTH
    )
    joined_values = jnp.concatenate([resident_values[0], fresh_values], 0).reshape(
        context + tokens_here, kv_here, HEAD_WIDTH
    )
    score = jnp.einsum(
        "tjgd,sjd->jgts", query_rows, joined_keys, preferred_element_type=jnp.float32
    ) * HEAD_WIDTH ** (-0.5)
    places = jnp.arange(context + tokens_here)
    rows = jnp.arange(tokens_here)
    allowed = (places[None, :] < context) | (places[None, :] - context <= rows[:, None])
    score = jnp.where(allowed, score, jnp.float32(-1e30))
    top_score = jnp.max(score, axis=-1, keepdims=True)
    weight = jnp.exp(score - top_score)
    probs = (weight / jnp.sum(weight, axis=-1, keepdims=True)).astype(jnp.bfloat16)
    attended = jnp.einsum(
        "jgts,sjd->tjgd", probs, joined_values, preferred_element_type=jnp.float32
    )
    return attended.reshape(tokens_here, -1).astype(jnp.bfloat16)


def swap_pair(x):
    return lax.ppermute(x, "tensor", [(0, 1), (1, 0)])


def per_device(
    queries,
    fresh_keys,
    fresh_values,
    resident_keys,
    resident_values,
    out_weight,
    residual,
    norm_gain,
    expert_ids,
    gates,
    w_gate,
    w_up,
    w_down,
):
    tokens_here = residual.shape[0]
    lane = lax.axis_index("tensor")
    half = D // lax.axis_size("tensor")
    groups = lax.axis_size("dp")
    attended = attend_local(queries, fresh_keys, fresh_values, resident_keys, resident_values)
    gathered = lax.all_gather(attended, "dp", axis=0, tiled=True)
    part = jnp.dot(gathered, out_weight, preferred_element_type=jnp.float32)
    part = part.reshape(groups, tokens_here, -1)
    mine = lax.all_to_all(part, "dp", split_axis=0, concat_axis=0, tiled=True)
    mine = mine.transpose(1, 0, 2).reshape(tokens_here, D)
    summed = mine + swap_pair(mine)
    hidden = residual.astype(jnp.float32) + summed
    mean_square = jnp.mean(hidden * hidden, axis=-1, keepdims=True)
    normed = (hidden * lax.rsqrt(mean_square + 1e-06) * norm_gain).astype(jnp.bfloat16)
    hidden_half = lax.dynamic_slice_in_dim(hidden, lane * half, half, 1)
    normed_half = lax.dynamic_slice_in_dim(normed, lane * half, half, 1)
    owners = lax.axis_size("dp") * lax.axis_size("expert")
    onehot = (expert_ids[:, :, None] == jnp.arange(owners)[None, None, :]).astype(jnp.int32)
    per_token = jnp.sum(onehot, axis=1)
    before = jnp.cumsum(per_token, axis=0) - per_token
    slot = jnp.sum(onehot * before[:, None, :], axis=-1)
    code = expert_ids * CAP + slot
    pick = (code[:, :, None] == jnp.arange(owners * CAP)[None, None, :]).astype(jnp.bfloat16)
    spread = jnp.sum(pick, axis=1)
    outgoing = jnp.einsum(
        "tr,tf->rf", spread, normed_half, preferred_element_type=jnp.float32
    ).astype(jnp.bfloat16)
    received = lax.all_to_all(
        outgoing.reshape(owners, CAP, half),
        ("dp", "expert"),
        split_axis=0,
        concat_axis=0,
        tiled=True,
    ).reshape(owners * CAP, half)
    other = swap_pair(received)
    first = jnp.where(lane == 0, received, other)
    second = jnp.where(lane == 0, other, received)
    flat = jnp.concatenate([first, second], axis=1)
    gate_part = jnp.dot(flat, w_gate[0], preferred_element_type=jnp.float32)
    up_part = jnp.dot(flat, w_up[0], preferred_element_type=jnp.float32)
    act = (jax.nn.silu(gate_part) * up_part).astype(jnp.bfloat16)
    result = jnp.dot(act, w_down[0], preferred_element_type=jnp.float32)
    own = lax.dynamic_slice_in_dim(result, lane * half, half, 1)
    theirs = lax.dynamic_slice_in_dim(result, (1 - lane) * half, half, 1)
    expert_out = (own + swap_pair(theirs)).astype(jnp.bfloat16)
    returned = lax.all_to_all(
        expert_out.reshape(owners, CAP, half),
        ("dp", "expert"),
        split_axis=0,
        concat_axis=0,
        tiled=True,
    ).reshape(owners * CAP, half)
    picked = jnp.einsum("tkr,rf->tkf", pick, returned, preferred_element_type=jnp.float32)
    moe = jnp.sum(gates[:, :, None] * picked, axis=1)
    return (hidden_half + moe).astype(jnp.bfloat16)


def solution(mesh):
    return jax.shard_map(
        per_device,
        mesh=mesh,
        in_specs=(
            P(("dp", "expert"), "tensor"),
            P(("dp", "expert"), "tensor"),
            P(("dp", "expert"), "tensor"),
            P(("dp", "expert"), None, "tensor"),
            P(("dp", "expert"), None, "tensor"),
            P("tensor", "dp"),
            P(("dp", "expert"), None),
            P(),
            P(("dp", "expert"), None),
            P(("dp", "expert"), None),
            P(("dp", "expert"), None, "tensor"),
            P(("dp", "expert"), None, "tensor"),
            P(("dp", "expert"), "tensor", None),
        ),
        out_specs=P(("dp", "expert"), "tensor"),
        check_vma=False,
    )
```

profile of v0, /device:TPU:2, one launch (start us, length us, event | category | flops | bytes accessed | tf_op | source)
XLA Modules:
  0.0 256.4 jit_solution(13007185668899665555)
XLA Ops:
  6.5 0.6 iota_add_fusion
  7.1 1.5 copy.47
  8.7 1.3 copy.48
  10.0 0.8 copy.62
  10.8 1.5 copy.44
  12.3 1.3 copy.45
  13.7 0.6 copy_bitcast_fusion.1
  14.3 0.8 fusion.27
  15.1 4.7 %fusion.48 = f32[2,8,64]{2,1,0:T(8,128)S(1)} fusion(pred[64,2112]{1,0:T(8,128)(4,1)S(1)} %fusion.27, bf16[64,2,128]{2,0,1:T(8,128)(2,1)} %get-tuple-element.9, bf16[2048,2,128]{2,0,1:T(8,128)(2,1)} %copy.48, bf16[64,2,8,128]{3,2,1,0:T(8,128)(2,1)S(1)} %bitcast.82), kind=kOutput, calls=%fused_computation.65 | convolution fusion | flops 564463680 | bytes 1482752 | tf_op jit(solution)/shard_map/sub | solution.py:31
  19.8 5.6 %fusion.14 = bf16[64,2,8,128]{3,0,2,1:T(8,128)(2,1)} fusion(f32[2,8,64]{2,1,0:T(8,128)S(1)} %fusion.48, bf16[64,2,128]{2,0,1:T(8,128)(2,1)} %get-tuple-element.10, bf16[2048,2,128]{2,0,1:T(8,128)(2,1)} %copy.45, pred[64,2112]{1,0:T(8,128)(4,1)S(1)} %fusion.27, bf16[64,2,128]{2,0,1:T(8,128)(2,1)} %get-tuple-element.9, ...), kind=kOutput, calls=%fused_computation.25 | convolution fusion | flops 1122569216 | bytes 2826240 | tf_op jit(solution)/shard_map/jgts,sjd->tjgd/dot_general | solution.py:33
  25.4 1.1 copy.51
  26.5 0.8 copy.78
  27.3 0.0 all-gather.2.cloned.1.call-update
  27.3 0.0 copy-start.10
  27.4 28.6 %all-gather.2.cloned.1.call-done = bf16[256,2048]{1,0:T(8,128)(2,1)} async-done(((bf16[64,2048]{1,0:T(8,128)(2,1)}), bf16[256,2048]{1,0:T(8,128)(2,1)}) %all-gather.2.cloned.1.call-update) | async-done | bytes 1048592 | tf_op jit(solution)/shard_map/all_gather | solution.py:63
  55.9 2.7 %fusion.51 = f32[256,512]{1,0:T(8,128)} fusion(bf16[256,2048]{1,0:T(8,128)(2,1)} %all-gather.2.cloned.1.call-done, bf16[2048,512]{1,0:T(8,128)(2,1)S(1)} %copy-done), kind=kOutput, calls=%fused_computation.66 | convolution fusion | flops 536870912 | bytes 3670016 | tf_op jit(solution)/shard_map/dot_general | solution.py:64
  58.7 5.3 %all-to-all-start = ((f32[4,64,512]{2,1,0:T(8,128)}), f32[4,64,512]{2,1,0:T(8,128)S(1)}, u32[]{:S(2)}, u32[]{:S(2)}) async-start(f32[4,64,512]{2,1,0:T(8,128)} %bitcast.8), calls=%async_computation | async-start | bytes 1048576 | tf_op jit(solution)/shard_map/all_to_all | solution.py:66
  64.0 0.1 copy.54
  64.0 6.5 %all-to-all-done = f32[4,64,512]{2,1,0:T(8,128)S(1)} async-done(((f32[4,64,512]{2,1,0:T(8,128)}), f32[4,64,512]{2,1,0:T(8,128)S(1)}, u32[]{:S(2)}, u32[]{:S(2)}) %all-to-all-start) | async-done | bytes 524320 | tf_op jit(solution)/shard_map/all_to_all | solution.py:66
  70.6 0.3 collective-permute-start
  70.9 0.1 convert_reduce_fusion
  71.1 0.1 reduce_window_sum.11
  71.2 1.2 select_reduce_fusion
  72.4 0.1 copy.55
  72.5 0.1 copy.56
  72.6 0.5 fusion.19
  73.2 1.2 multiply_reduce_fusion.1
  74.4 1.8 convolution_convert_fusion
  76.2 3.7 %reshape.67 = bf16[128,6,1024]{2,1,0:T(8,128)(2,1)} reshape(bf16[768,1024]{1,0:T(8,128)(2,1)} %convolution_convert_fusion) | data formatting | bytes 3145728 | tf_op jit(solution)/shard_map/reshape | solution.py:86
  79.9 64.9 %all_to_all.15 = bf16[128,6,1024]{2,1,0:T(8,128)(2,1)} all-to-all(bf16[128,6,1024]{2,1,0:T(8,128)(2,1)} %reshape.67), channel_id=1, replica_groups=mesh['dp'=4,'expert'=32,'tensor'=2] {'dp','expert'}, dimensions={0} | all-to-all | bytes 3145728 | tf_op jit(solution)/shard_map/all_to_all | solution.py:85
  144.8 3.7 %reshape.68 = bf16[768,1024]{1,0:T(8,128)(2,1)} reshape(bf16[128,6,1024]{2,1,0:T(8,128)(2,1)} %all_to_all.15) | data formatting | bytes 3145728 | tf_op jit(solution)/shard_map/reshape | solution.py:91
  148.5 3.7 %collective-permute-done.1 = bf16[768,1024]{1,0:T(8,128)(2,1)} collective-permute-done((bf16[768,1024]{1,0:T(8,128)(2,1)}, bf16[768,1024]{1,0:T(8,128)(2,1)}, u32[]{:S(2)}, u32[]{:S(2)}) %collective-permute-start.1) | collective-permute-done | bytes 1572896 | tf_op jit(solution)/shard_map/ppermute | solution.py:40
  152.3 2.1 broadcast_select_fusion.1
  154.4 1.2 copy-done.2
  155.6 0.4 copy-done.3
  156.0 2.8 %fusion.6 = f32[768,384]{1,0:T(8,128)} fusion(bf16[768,1024]{1,0:T(8,128)(2,1)S(1)} %get-tuple-element.8, bf16[768,1024]{1,0:T(8,128)(2,1)S(1)} %get-tuple-element.7, bf16[1,2048,384]{2,1,0:T(8,128)(2,1)S(1)} %copy-done.13), kind=kOutput, calls=%fused_computation.12 | convolution fusion | flops 1214251008 | bytes 5898240 | tf_op jit(solution)/shard_map/dot_general | solution.py:97
  158.8 9.3 %fusion.8 = f32[768,2048]{1,0:T(8,128)} fusion(bf16[1,384,2048]{2,1,0:T(8,128)(2,1)} %param.25, f32[768,384]{1,0:T(8,128)} %fusion.6, bf16[768,1024]{1,0:T(8,128)(2,1)} %copy-done.3, bf16[768,1024]{1,0:T(8,128)(2,1)} %copy-done.2, bf16[1,2048,384]{2,1,0:T(8,128)(2,1)} %param.23), kind=kOutput, calls=%fused_computation.15 | convolution fusion | flops 2423980032 | bytes 13762560 | tf_op jit(solution)/shard_map/dot_general | solution.py:99
  168.0 2.3 constant_dynamic-slice_fusion
  170.3 0.2 collective-permute-start.2
  170.5 5.5 %collective-permute-done.2 = f32[768,1024]{1,0:T(8,128)S(1)} collective-permute-done((f32[768,1024]{1,0:T(8,128)S(1)}, f32[768,1024]{1,0:T(8,128)S(1)}, u32[]{:S(2)}, u32[]{:S(2)}) %collective-permute-start.2) | collective-permute-done | bytes 3145760 | tf_op jit(solution)/shard_map/ppermute | solution.py:40
  176.1 1.7 add_convert_fusion
  177.7 3.7 %reshape.69 = bf16[128,6,1024]{2,1,0:T(8,128)(2,1)} reshape(bf16[768,1024]{1,0:T(8,128)(2,1)} %add_convert_fusion) | data formatting | bytes 3145728 | tf_op jit(solution)/shard_map/reshape | solution.py:104
  181.4 9.0 %all-to-all-start.2 = ((bf16[128,6,1024]{2,1,0:T(8,128)(2,1)}), bf16[128,6,1024]{2,1,0:T(8,128)(2,1)}, u32[]{:S(2)}, u32[]{:S(2)}) async-start(bf16[128,6,1024]{2,1,0:T(8,128)(2,1)} %reshape.69), calls=%async_computation.2 | async-start | bytes 4194304 | tf_op jit(solution)/shard_map/all_to_all | solution.py:103
  190.5 0.1 copy.53
  190.6 51.7 %all-to-all-done.2 = bf16[128,6,1024]{2,1,0:T(8,128)(2,1)} async-done(((bf16[128,6,1024]{2,1,0:T(8,128)(2,1)}), bf16[128,6,1024]{2,1,0:T(8,128)(2,1)}, u32[]{:S(2)}, u32[]{:S(2)}) %all-to-all-start.2) | async-done | bytes 1572896 | tf_op jit(solution)/shard_map/all_to_all | solution.py:103
  242.3 3.7 %reshape.73 = bf16[768,1024,1]{1,0,2:T(8,128)(2,1)} reshape(bf16[128,6,1024]{2,1,0:T(8,128)(2,1)} %all-to-all-done.2) | data formatting | bytes 3145728 | tf_op jit(solution)/shard_map/reshape | solution.py:109
  246.0 2.8 %multiply_reduce_fusion = f32[64,1024]{1,0:T(8,128)S(1)} fusion(bf16[768,1024,1]{1,0,2:T(8,128)(2,1)} %reshape.73, f32[64,8]{1,0:T(8,128)S(1)} %copy.53, s32[64,8]{1,0:T(8,128)S(1)} %copy.56), kind=kOutput, calls=%fused_computation.11 | convolution fusion | flops 806682624 | bytes 1839104 | tf_op jit(solution)/shard_map/tkr,rf->tkf/dot_general | solution.py:110
  248.8 0.7 add_convert_fusion.1
  (34 shorter events, 0.1 us)
Async XLA Ops:
  6.5 49.4 %copy-start = (bf16[2048,512]{1,0:T(8,128)(2,1)S(1)}, bf16[2048,512]{1,0:T(8,128)(2,1)}, u32[]{:S(2)}) copy-start(bf16[2048,512]{1,0:T(8,128)(2,1)} %param.18) | copy-start | bytes 6291460
  6.5 49.4 %all-gather.2.cloned.1.call-start = ((), (), s32[]{:S(2)}) async-start(), calls=%async_computation.3 | async-start | bytes 1310720 | tf_op jit(solution)/shard_map/all_gather | solution.py:63
  7.1 2.9 %copy-start.5 = (bf16[64,2048]{1,0:T(8,128)(2,1)S(1)}, bf16[64,2048]{1,0:T(8,128)(2,1)}, u32[]{:S(2)}) copy-start(bf16[64,2048]{1,0:T(8,128)(2,1)} %param.13) | copy-start | bytes 786436
  10.8 2.9 %copy-start.8 = (bf16[64,256]{1,0:T(8,128)(2,1)S(1)}, bf16[64,256]{1,0:T(8,128)(2,1)}, u32[]{:S(2)}) copy-start(bf16[64,256]{1,0:T(8,128)(2,1)} %param.15) | copy-start | bytes 98308
  10.8 2.9 %copy-start.9 = (bf16[64,256]{1,0:T(8,128)(2,1)S(1)}, bf16[64,256]{1,0:T(8,128)(2,1)}, u32[]{:S(2)}) copy-start(bf16[64,256]{1,0:T(8,128)(2,1)} %param.14) | copy-start | bytes 98308
  10.8 4.3 %copy-start.6 = (bf16[8,8,16,128]{3,2,1,0:T(8,128)(2,1)S(1)}, bf16[8,8,16,128]{3,2,1,0:T(8,128)(2,1)}, u32[]{:S(2)}) copy-start(bf16[8,8,16,128]{3,2,1,0:T(8,128)(2,1)} %copy.62) | copy-start | bytes 786436
  15.1 4.7 %copy-start.4 = (bf16[2048,2,128]{2,0,1:T(8,128)(2,1)S(1)}, bf16[2048,2,128]{2,0,1:T(8,128)(2,1)}, u32[]{:S(2)}) copy-start(bf16[2048,2,128]{2,0,1:T(8,128)(2,1)} %copy.48) | copy-start | bytes 3145732
  27.3 36.6 %copy-start.10 = (s32[64,8]{0,1:T(8,128)S(1)}, s32[64,8]{0,1:T(8,128)}, u32[]{:S(2)}) copy-start(s32[64,8]{0,1:T(8,128)} %param.21) | copy-start | bytes 6148
  58.7 13.9 %copy-start.12 = (f32[2048]{0:T(1024)S(1)}, f32[2048]{0:T(1024)}, u32[]{:S(2)}) copy-start(f32[2048]{0:T(1024)} %param.20) | copy-start | bytes 24580
  58.7 14.5 %copy-start.7 = (bf16[64,2048]{1,0:T(8,128)(2,1)S(1)}, bf16[64,2048]{1,0:T(8,128)(2,1)}, u32[]{:S(2)}) copy-start(bf16[64,2048]{1,0:T(8,128)(2,1)} %param.19) | copy-start | bytes 786436
  58.7 11.9 %all-to-all-start = ((f32[4,64,512]{2,1,0:T(8,128)}), f32[4,64,512]{2,1,0:T(8,128)S(1)}, u32[]{:S(2)}, u32[]{:S(2)}) async-start(f32[4,64,512]{2,1,0:T(8,128)} %bitcast.8), calls=%async_computation | async-start | bytes 1048576 | tf_op jit(solution)/shard_map/all_to_all | solution.py:66
  70.6 2.5 collective-permute-start
  148.5 3.8 %collective-permute-start.1 = (bf16[768,1024]{1,0:T(8,128)(2,1)}, bf16[768,1024]{1,0:T(8,128)(2,1)}, u32[]{:S(2)}, u32[]{:S(2)}) collective-permute-start(bf16[768,1024]{1,0:T(8,128)(2,1)} %reshape.68), channel_id=1, source_target_pairs={{0,1},{1,0},{2,3},{3,2},{4,5},{5,4},{6,7},{7,6},{8,9},{9,8},{10,11... | collective-permute-start | bytes 4718600 | tf_op jit(solution)/shard_map/ppermute | solution.py:40
  148.5 7.5 %copy-start.13 = (bf16[1,2048,384]{2,1,0:T(8,128)(2,1)S(1)}, bf16[1,2048,384]{2,1,0:T(8,128)(2,1)}, u32[]{:S(2)}) copy-start(bf16[1,2048,384]{2,1,0:T(8,128)(2,1)} %param.24) | copy-start | bytes 4718596
  154.3 1.2 copy-start.2
  154.4 1.6 copy-start.3
  168.0 8.0 %copy-start.1 = (f32[768,2048]{1,0:T(8,128)S(1)}, f32[768,2048]{1,0:T(8,128)}, u32[]{:S(2)}) copy-start(f32[768,2048]{1,0:T(8,128)} %fusion.8) | copy-start | bytes 18874372
  170.3 5.7 %collective-permute-start.2 = (f32[768,1024]{1,0:T(8,128)S(1)}, f32[768,1024]{1,0:T(8,128)S(1)}, u32[]{:S(2)}, u32[]{:S(2)}) collective-permute-start(f32[768,1024]{1,0:T(8,128)S(1)} %constant_dynamic-slice_fusion), channel_id=1, source_target_pairs={{0,1},{1,0},{2,3},{3,2},{4,5},{5,4},{6,7},{7,6},{8,9},{9,8},{10,11... | collective-permute-start | bytes 9437192 | tf_op jit(solution)/shard_map/ppermute | solution.py:40
  181.4 9.0 %copy-start.11 = (f32[64,8]{0,1:T(8,128)S(1)}, f32[64,8]{0,1:T(8,128)}, u32[]{:S(2)}) copy-start(f32[64,8]{0,1:T(8,128)} %param.22) | copy-start | bytes 6148
  181.4 60.9 %all-to-all-start.2 = ((bf16[128,6,1024]{2,1,0:T(8,128)(2,1)}), bf16[128,6,1024]{2,1,0:T(8,128)(2,1)}, u32[]{:S(2)}, u32[]{:S(2)}) async-start(bf16[128,6,1024]{2,1,0:T(8,128)(2,1)} %reshape.69), calls=%async_computation.2 | async-start | bytes 4194304 | tf_op jit(solution)/shard_map/all_to_all | solution.py:103
Sparse Core Ops, SparseCore 0:
  27.5 28.4 all-gather.1
where the time goes:
time: 257 us; the launch traced here: 256 us
  waiting for transfers between devices  96.2 us (37%)
  blocking collectives  64.9 us (25%)
  matrix products  29.7 us (12%)
  local copies, waits for them, and re-layouts  28.1 us (11%)
  starting transfers between devices  14.8 us (6%)
  between operations  13.6 us (5%)
  other arithmetic  9.14 us (4%)
    all_to_all x1, blocking collectives, per_device(): lax.all_to_all(outgoing.reshape(owners, CAP, half), ('dp', 'expert'), spl...  64.9 us
    all_to_all x1, waiting for transfers between devices, per_device(): lax.all_to_all(expert_out.reshape(owners, CAP, half), ('dp', 'expert'), s...  51.7 us
    all_gather x1, waiting for transfers between devices, per_device(): gathered = lax.all_gather(attended, 'dp', axis=0, tiled=True)  28.6 us
    dot_general x1, matrix products, per_device(): result = jnp.dot(act, w_down[0], preferred_element_type=jnp.float32)  9.28 us
    ppermute x3, waiting for transfers between devices, swap_pair(): return lax.ppermute(x, 'tensor', [(0, 1), (1, 0)])  9.27 us
    all_to_all x1, starting transfers between devices, per_device(): lax.all_to_all(expert_out.reshape(owners, CAP, half), ('dp', 'expert'), s...  9.03 us
    all_to_all x1, waiting for transfers between devices, per_device(): mine = lax.all_to_all(part, 'dp', split_axis=0, concat_axis=0, tiled=True)  6.54 us
    unnamed x34, local copies, waits for them, and re-layouts  6.45 us
  transfers between devices with their start and end apart: 6, of which 5 were waited for; matrix products, arithmetic and copies ran while one was open for 1% of the time, Pallas kernels for 0%

commit v1 on v0

--- a/solution.py
+++ b/solution.py
@@ -60,7 +60,13 @@
     half = D // lax.axis_size("tensor")
     groups = lax.axis_size("dp")
     attended = attend_local(queries, fresh_keys, fresh_values, resident_keys, resident_values)
-    gathered = lax.all_gather(attended, "dp", axis=0, tiled=True)
+
+    def _match_column(x_part, device_axis):
+        return jnp.concatenate(
+            lax.all_to_all(jnp.stack([x_part] * lax.psum(1, device_axis), 0), device_axis, 0, 0), 0
+        )
+
+    gathered = _match_column(attended, "dp")
     part = jnp.dot(gathered, out_weight, preferred_element_type=jnp.float32)
     part = part.reshape(groups, tokens_here, -1)
     mine = lax.all_to_all(part, "dp", split_axis=0, concat_axis=0, tiled=True)

time: 257 us -> 234 us (0.911)
  waiting for transfers between devices: 96.2 us -> 68.1 us
  blocking collectives: 64.9 us -> 84.8 us
  between operations: 13.6 us -> 0.21 us
    all_gather x1 -> x0, waiting for transfers between devices: 28.6 us -> none  [per_device(): gathered = lax.all_gather(attended, 'dp', axis=0, tiled=True)]
    all_to_all x0 -> x1, blocking collectives: none -> 18.3 us  [_match_column(): lax.all_to_all(jnp.stack([x_part] * lax.psum(1, device_axis), 0), device_...]
  transfers between devices with their start and end apart: 6 -> 5, of which waited for: 5 -> 4; matrix products, arithmetic and copies ran while one was open for 1% -> 1% of each run, Pallas kernels for 0% -> 0%
where the time goes in v1:
time: 234 us; the launch traced here: 233 us
  blocking collectives  84.8 us (36%)
  waiting for transfers between devices  68.1 us (29%)
  matrix products  28.4 us (12%)
  local copies, waits for them, and re-layouts  27.5 us (12%)
  starting transfers between devices  14.6 us (6%)
  other arithmetic  9.13 us (4%)
    all_to_all x1, blocking collectives, per_device(): lax.all_to_all(outgoing.reshape(owners, CAP, half), ('dp', 'expert'), spl...  66.6 us
    all_to_all x1, waiting for transfers between devices, per_device(): lax.all_to_all(expert_out.reshape(owners, CAP, half), ('dp', 'expert'), s...  51.7 us
    all_to_all x1, blocking collectives, _match_column(): lax.all_to_all(jnp.stack([x_part] * lax.psum(1, device_axis), 0), device_...  18.3 us
    dot_general x1, matrix products, per_device(): result = jnp.dot(act, w_down[0], preferred_element_type=jnp.float32)  9.28 us
    ppermute x3, waiting for transfers between devices, swap_pair(): return lax.ppermute(x, 'tensor', [(0, 1), (1, 0)])  9.27 us
    all_to_all x1, starting transfers between devices, per_device(): lax.all_to_all(expert_out.reshape(owners, CAP, half), ('dp', 'expert'), s...  9.03 us
    all_to_all x1, waiting for transfers between devices, per_device(): mine = lax.all_to_all(part, 'dp', split_axis=0, concat_axis=0, tiled=True)  7.05 us
    unnamed x34, local copies, waits for them, and re-layouts  5.73 us
  transfers between devices with their start and end apart: 5, of which 4 were waited for; matrix products, arithmetic and copies ran while one was open for 1% of the time, Pallas kernels for 0%

profile of v1, /device:TPU:2, one launch (start us, length us, event | category | flops | bytes accessed | tf_op | source)
XLA Modules:
  0.0 232.7 jit_solution(9801580326967590014)
XLA Ops:
  0.0 0.6 iota_add_fusion
  0.6 1.5 copy.46
  2.1 1.3 copy.47
  3.5 0.8 copy.61
  4.3 1.5 copy.43
  5.8 1.3 copy.44
  7.1 0.6 copy_bitcast_fusion.1
  7.8 0.8 fusion.29
  8.6 4.7 %fusion.50 = f32[2,8,64]{2,1,0:T(8,128)S(1)} fusion(pred[64,2112]{1,0:T(8,128)(4,1)S(1)} %fusion.29, bf16[64,2,128]{2,0,1:T(8,128)(2,1)} %get-tuple-element.9, bf16[2048,2,128]{2,0,1:T(8,128)(2,1)} %copy.47, bf16[64,2,8,128]{3,2,1,0:T(8,128)(2,1)S(1)} %bitcast.83), kind=kOutput, calls=%fused_computation.67 | convolution fusion | flops 564463680 | bytes 1482752 | tf_op jit(solution)/shard_map/sub | solution.py:31
  13.2 5.6 %fusion.16 = bf16[64,2,8,128]{3,0,2,1:T(8,128)(2,1)} fusion(f32[2,8,64]{2,1,0:T(8,128)S(1)} %fusion.50, bf16[64,2,128]{2,0,1:T(8,128)(2,1)} %get-tuple-element.10, bf16[2048,2,128]{2,0,1:T(8,128)(2,1)} %copy.44, pred[64,2112]{1,0:T(8,128)(4,1)S(1)} %fusion.29, bf16[64,2,128]{2,0,1:T(8,128)(2,1)} %get-tuple-element.9, ...), kind=kOutput, calls=%fused_computation.27 | convolution fusion | flops 1122569216 | bytes 2826240 | tf_op jit(solution)/shard_map/jgts,sjd->tjgd/dot_general | solution.py:33
  18.9 1.1 copy.50
  20.0 0.1 copy.77
  20.1 0.1 stack.2
  20.2 18.3 %all_to_all.20 = bf16[4,64,2048]{2,1,0:T(8,128)(2,1)S(1)} all-to-all(bf16[4,64,2048]{2,1,0:T(8,128)(2,1)S(1)} %stack.2), channel_id=1, replica_groups=mesh['dp'=4,'expert'=32,'tensor'=2] {'dp'}, dimensions={0} | all-to-all | bytes 2097152 | tf_op jit(solution)/shard_map/all_to_all | solution.py:66
  38.5 1.5 fusion.6
  40.0 5.0 %all-to-all-start.1 = ((f32[4,64,512]{2,1,0:T(8,128)}), f32[4,64,512]{2,1,0:T(8,128)S(1)}, u32[]{:S(2)}, u32[]{:S(2)}) async-start(f32[4,64,512]{2,1,0:T(8,128)} %fusion.6), calls=%async_computation.1 | async-start | bytes 1048576 | tf_op jit(solution)/shard_map/all_to_all | solution.py:72
  45.0 0.1 copy.53
  45.1 7.0 %all-to-all-done.1 = f32[4,64,512]{2,1,0:T(8,128)S(1)} async-done(((f32[4,64,512]{2,1,0:T(8,128)}), f32[4,64,512]{2,1,0:T(8,128)S(1)}, u32[]{:S(2)}, u32[]{:S(2)}) %all-to-all-start.1) | async-done | bytes 524320 | tf_op jit(solution)/shard_map/all_to_all | solution.py:72
  52.2 0.3 collective-permute-start
  52.4 0.1 convert_reduce_fusion
  52.6 0.1 reduce_window_sum.11
  52.7 1.2 select_reduce_fusion
  54.0 0.1 copy.54
  54.0 0.1 copy.55
  54.1 0.0 copy-done.12
  54.1 0.5 fusion.21
  54.7 1.2 multiply_reduce_fusion.1
  55.9 1.8 convolution_convert_fusion
  57.7 3.7 %reshape.70 = bf16[128,6,1024]{2,1,0:T(8,128)(2,1)} reshape(bf16[768,1024]{1,0:T(8,128)(2,1)} %convolution_convert_fusion) | data formatting | bytes 3145728 | tf_op jit(solution)/shard_map/reshape | solution.py:92
  61.4 66.6 %all_to_all.21 = bf16[128,6,1024]{2,1,0:T(8,128)(2,1)} all-to-all(bf16[128,6,1024]{2,1,0:T(8,128)(2,1)} %reshape.70), channel_id=1, replica_groups=mesh['dp'=4,'expert'=32,'tensor'=2] {'dp','expert'}, dimensions={0} | all-to-all | bytes 3145728 | tf_op jit(solution)/shard_map/all_to_all | solution.py:91
  128.0 3.7 %reshape.71 = bf16[768,1024]{1,0:T(8,128)(2,1)} reshape(bf16[128,6,1024]{2,1,0:T(8,128)(2,1)} %all_to_all.21) | data formatting | bytes 3145728 | tf_op jit(solution)/shard_map/reshape | solution.py:97
  131.7 3.7 %collective-permute-done.1 = bf16[768,1024]{1,0:T(8,128)(2,1)} collective-permute-done((bf16[768,1024]{1,0:T(8,128)(2,1)}, bf16[768,1024]{1,0:T(8,128)(2,1)}, u32[]{:S(2)}, u32[]{:S(2)}) %collective-permute-start.1) | collective-permute-done | bytes 1572896 | tf_op jit(solution)/shard_map/ppermute | solution.py:40
  135.5 2.1 broadcast_select_fusion.1
  137.6 1.2 copy-done.2
  138.8 0.4 copy-done.3
  139.2 2.8 %fusion.8 = f32[768,384]{1,0:T(8,128)} fusion(bf16[768,1024]{1,0:T(8,128)(2,1)S(1)} %get-tuple-element.8, bf16[768,1024]{1,0:T(8,128)(2,1)S(1)} %get-tuple-element.7, bf16[1,2048,384]{2,1,0:T(8,128)(2,1)S(1)} %copy-done.13), kind=kOutput, calls=%fused_computation.14 | convolution fusion | flops 1214251008 | bytes 5898240 | tf_op jit(solution)/shard_map/dot_general | solution.py:103
  142.0 9.3 %fusion.10 = f32[768,2048]{1,0:T(8,128)} fusion(bf16[1,384,2048]{2,1,0:T(8,128)(2,1)} %param.25, f32[768,384]{1,0:T(8,128)} %fusion.8, bf16[768,1024]{1,0:T(8,128)(2,1)} %copy-done.3, bf16[768,1024]{1,0:T(8,128)(2,1)} %copy-done.2, bf16[1,2048,384]{2,1,0:T(8,128)(2,1)} %param.23), kind=kOutput, calls=%fused_computation.17 | convolution fusion | flops 2423980032 | bytes 13762560 | tf_op jit(solution)/shard_map/dot_general | solution.py:105
  151.3 2.3 constant_dynamic-slice_fusion
  153.6 0.2 collective-permute-start.2
  153.8 5.5 %collective-permute-done.2 = f32[768,1024]{1,0:T(8,128)S(1)} collective-permute-done((f32[768,1024]{1,0:T(8,128)S(1)}, f32[768,1024]{1,0:T(8,128)S(1)}, u32[]{:S(2)}, u32[]{:S(2)}) %collective-permute-start.2) | collective-permute-done | bytes 3145760 | tf_op jit(solution)/shard_map/ppermute | solution.py:40
  159.3 1.7 add_convert_fusion
  161.0 3.7 %reshape.72 = bf16[128,6,1024]{2,1,0:T(8,128)(2,1)} reshape(bf16[768,1024]{1,0:T(8,128)(2,1)} %add_convert_fusion) | data formatting | bytes 3145728 | tf_op jit(solution)/shard_map/reshape | solution.py:110
  164.7 9.0 %all-to-all-start.3 = ((bf16[128,6,1024]{2,1,0:T(8,128)(2,1)}), bf16[128,6,1024]{2,1,0:T(8,128)(2,1)}, u32[]{:S(2)}, u32[]{:S(2)}) async-start(bf16[128,6,1024]{2,1,0:T(8,128)(2,1)} %reshape.72), calls=%async_computation.3 | async-start | bytes 4194304 | tf_op jit(solution)/shard_map/all_to_all | solution.py:109
  173.7 0.1 copy.52
  173.8 51.7 %all-to-all-done.3 = bf16[128,6,1024]{2,1,0:T(8,128)(2,1)} async-done(((bf16[128,6,1024]{2,1,0:T(8,128)(2,1)}), bf16[128,6,1024]{2,1,0:T(8,128)(2,1)}, u32[]{:S(2)}, u32[]{:S(2)}) %all-to-all-start.3) | async-done | bytes 1572896 | tf_op jit(solution)/shard_map/all_to_all | solution.py:109
  225.6 3.7 %reshape.77 = bf16[768,1024,1]{1,0,2:T(8,128)(2,1)} reshape(bf16[128,6,1024]{2,1,0:T(8,128)(2,1)} %all-to-all-done.3) | data formatting | bytes 3145728 | tf_op jit(solution)/shard_map/reshape | solution.py:115
  229.3 2.8 %multiply_reduce_fusion = f32[64,1024]{1,0:T(8,128)S(1)} fusion(bf16[768,1024,1]{1,0,2:T(8,128)(2,1)} %reshape.77, f32[64,8]{1,0:T(8,128)S(1)} %copy.52, s32[64,8]{1,0:T(8,128)S(1)} %copy.55), kind=kOutput, calls=%fused_computation.13 | convolution fusion | flops 806682624 | bytes 1839104 | tf_op jit(solution)/shard_map/tkr,rf->tkf/dot_general | solution.py:116
  232.0 0.7 add_convert_fusion.1
  (33 shorter events, 0.1 us)
Async XLA Ops:
  0.0 38.5 %copy-start = (bf16[2048,512]{1,0:T(8,128)(2,1)S(1)}, bf16[2048,512]{1,0:T(8,128)(2,1)}, u32[]{:S(2)}) copy-start(bf16[2048,512]{1,0:T(8,128)(2,1)} %param.18) | copy-start | bytes 6291460
  0.6 2.9 %copy-start.5 = (bf16[64,2048]{1,0:T(8,128)(2,1)S(1)}, bf16[64,2048]{1,0:T(8,128)(2,1)}, u32[]{:S(2)}) copy-start(bf16[64,2048]{1,0:T(8,128)(2,1)} %param.13) | copy-start | bytes 786436
  4.2 2.9 %copy-start.8 = (bf16[64,256]{1,0:T(8,128)(2,1)S(1)}, bf16[64,256]{1,0:T(8,128)(2,1)}, u32[]{:S(2)}) copy-start(bf16[64,256]{1,0:T(8,128)(2,1)} %param.15) | copy-start | bytes 98308
  4.2 2.9 %copy-start.9 = (bf16[64,256]{1,0:T(8,128)(2,1)S(1)}, bf16[64,256]{1,0:T(8,128)(2,1)}, u32[]{:S(2)}) copy-start(bf16[64,256]{1,0:T(8,128)(2,1)} %param.14) | copy-start | bytes 98308
  4.3 4.3 %copy-start.6 = (bf16[8,8,16,128]{3,2,1,0:T(8,128)(2,1)S(1)}, bf16[8,8,16,128]{3,2,1,0:T(8,128)(2,1)}, u32[]{:S(2)}) copy-start(bf16[8,8,16,128]{3,2,1,0:T(8,128)(2,1)} %copy.61) | copy-start | bytes 786436
  8.6 4.7 %copy-start.4 = (bf16[2048,2,128]{2,0,1:T(8,128)(2,1)S(1)}, bf16[2048,2,128]{2,0,1:T(8,128)(2,1)}, u32[]{:S(2)}) copy-start(bf16[2048,2,128]{2,0,1:T(8,128)(2,1)} %copy.47) | copy-start | bytes 3145732
  38.5 6.5 %copy-start.10 = (s32[64,8]{0,1:T(8,128)S(1)}, s32[64,8]{0,1:T(8,128)}, u32[]{:S(2)}) copy-start(s32[64,8]{0,1:T(8,128)} %param.21) | copy-start | bytes 6148
  40.0 14.2 %copy-start.12 = (f32[2048]{0:T(1024)S(1)}, f32[2048]{0:T(1024)}, u32[]{:S(2)}) copy-start(f32[2048]{0:T(1024)} %param.20) | copy-start | bytes 24580
  40.0 14.7 %copy-start.7 = (bf16[64,2048]{1,0:T(8,128)(2,1)S(1)}, bf16[64,2048]{1,0:T(8,128)(2,1)}, u32[]{:S(2)}) copy-start(bf16[64,2048]{1,0:T(8,128)(2,1)} %param.19) | copy-start | bytes 786436
  40.0 12.2 %all-to-all-start.1 = ((f32[4,64,512]{2,1,0:T(8,128)}), f32[4,64,512]{2,1,0:T(8,128)S(1)}, u32[]{:S(2)}, u32[]{:S(2)}) async-start(f32[4,64,512]{2,1,0:T(8,128)} %fusion.6), calls=%async_computation.1 | async-start | bytes 1048576 | tf_op jit(solution)/shard_map/all_to_all | solution.py:72
  52.2 2.5 %collective-permute-start = (f32[64,2048]{1,0:T(8,128)S(1)}, f32[64,2048]{1,0:T(8,128)}, u32[]{:S(2)}, u32[]{:S(2)}) collective-permute-start(f32[64,2048]{1,0:T(8,128)S(1)} %bitcast.78), channel_id=1, source_target_pairs={{0,1},{1,0},{2,3},{3,2},{4,5},{5,4},{6,7},{7,6},{8,9},{9,8},{10,11... | collective-permute-start | bytes 1572872 | tf_op jit(solution)/shard_map/ppermute | solution.py:40
  131.7 3.8 %collective-permute-start.1 = (bf16[768,1024]{1,0:T(8,128)(2,1)}, bf16[768,1024]{1,0:T(8,128)(2,1)}, u32[]{:S(2)}, u32[]{:S(2)}) collective-permute-start(bf16[768,1024]{1,0:T(8,128)(2,1)} %reshape.71), channel_id=1, source_target_pairs={{0,1},{1,0},{2,3},{3,2},{4,5},{5,4},{6,7},{7,6},{8,9},{9,8},{10,11... | collective-permute-start | bytes 4718600 | tf_op jit(solution)/shard_map/ppermute | solution.py:40
  131.7 7.5 %copy-start.13 = (bf16[1,2048,384]{2,1,0:T(8,128)(2,1)S(1)}, bf16[1,2048,384]{2,1,0:T(8,128)(2,1)}, u32[]{:S(2)}) copy-start(bf16[1,2048,384]{2,1,0:T(8,128)(2,1)} %param.24) | copy-start | bytes 4718596
  137.6 1.2 copy-start.2
  137.6 1.6 copy-start.3
  151.3 8.0 %copy-start.1 = (f32[768,2048]{1,0:T(8,128)S(1)}, f32[768,2048]{1,0:T(8,128)}, u32[]{:S(2)}) copy-start(f32[768,2048]{1,0:T(8,128)} %fusion.10) | copy-start | bytes 18874372
  153.6 5.7 %collective-permute-start.2 = (f32[768,1024]{1,0:T(8,128)S(1)}, f32[768,1024]{1,0:T(8,128)S(1)}, u32[]{:S(2)}, u32[]{:S(2)}) collective-permute-start(f32[768,1024]{1,0:T(8,128)S(1)} %constant_dynamic-slice_fusion), channel_id=1, source_target_pairs={{0,1},{1,0},{2,3},{3,2},{4,5},{5,4},{6,7},{7,6},{8,9},{9,8},{10,11... | collective-permute-start | bytes 9437192 | tf_op jit(solution)/shard_map/ppermute | solution.py:40
  164.7 9.0 %copy-start.11 = (f32[64,8]{0,1:T(8,128)S(1)}, f32[64,8]{0,1:T(8,128)}, u32[]{:S(2)}) copy-start(f32[64,8]{0,1:T(8,128)} %param.22) | copy-start | bytes 6148
  164.7 60.9 %all-to-all-start.3 = ((bf16[128,6,1024]{2,1,0:T(8,128)(2,1)}), bf16[128,6,1024]{2,1,0:T(8,128)(2,1)}, u32[]{:S(2)}, u32[]{:S(2)}) async-start(bf16[128,6,1024]{2,1,0:T(8,128)(2,1)} %reshape.72), calls=%async_computation.3 | async-start | bytes 4194304 | tf_op jit(solution)/shard_map/all_to_all | solution.py:109
